TPU v7x, 32 devices: a whole 2x2x4 slice. The times are simulated.
32 devices in a mesh: row: 4 (over y, core), col: 8 (over z, x).
Axes of the slice: x: 2, y: 2, z: 4, core: 2. Of those that a mesh axis runs over, the one named last changes fastest.
Arguments:
- node_feats: bfloat16 [8192, 512], P(('row', 'col')), may hold values from -6 to 6
- w_gate: bfloat16 [512, 2048], P(None, ('row', 'col')), may hold values from -0.25 to 0.25
- w_up: bfloat16 [512, 2048], P(None, ('row', 'col')), may hold values from -0.25 to 0.25
- w_down: bfloat16 [2048, 512], P(('row', 'col')), may hold values from -0.125 to 0.125
- tile_src: int32 [512], P(('row', 'col')), may hold values from 0 to 3
- tile_dst: int32 [512], P(('row', 'col')), may hold values from 0 to 1
- tile_mask: int32 [512, 512, 512], P(('row', 'col')), may hold values 0 or 1
- tile_count: int32 [32], P(('row', 'col')), may hold values from 1 to 16, as said below
Outputs:
- entry_loss: float32 [], replicated
- grad_gate: float32 [512, 2048], P(None, ('row', 'col'))
- grad_up: float32 [512, 2048], P(None, ('row', 'col'))
- grad_down: float32 [2048, 512], P(('row', 'col'))
Inputs may be any that keep to these rules, and one draw needn't show every extreme that they name: `tile_count`: some device has all 16 slots live.
All inputs are finite; a program needn't handle non-finite values. No bound on the sum of `tile_mask` on one device may be relied on, other than what follows from the above.
Results may differ from a plain program's by a relative error of at most 0.01.
Values may be sent and summed in bfloat16 or wider, within the bound.
A program may use at most 128 MiB of HBM per device.

v0:
```python
import functools
import math

import jax
import jax.numpy as jnp
from jax import lax
from jax.experimental import pallas as pl
from jax.experimental.pallas import tpu as pltpu
from jax.sharding import PartitionSpec as P

BLOCK = 512
CHUNKS = 4
F32 = jnp.float32
BF16 = jnp.bfloat16
NT = (((1,), (1,)), ((), ()))
TN = (((0,), (0,)), ((), ()))


def dot_nt(a, b):
    return lax.dot_general(a, b, NT, preferred_element_type=F32)


def dot_tn(a, b):
    return lax.dot_general(a, b, TN, preferred_element_type=F32)


def halve(x, op, rows):
    while x.shape[0] > rows:
        half = x.shape[0] // 2
        x = op(x[:half], x[half:])
    return x


def tile_kernel(half_scale, count_ref, src_id, dst_id, src_ref, dst_ref, mask_ref,
                src_out, dst_out, loss_out, src_acc, dst_acc, grad_buf, hinge_acc, log_acc):
    slot = pl.program_id(0)
    width = src_ref.shape[1]

    @pl.when(slot == 0)
    def _():
        src_acc[...] = jnp.zeros_like(src_acc)
        dst_acc[...] = jnp.zeros_like(dst_acc)
        hinge_acc[...] = jnp.zeros_like(hinge_acc)
        log_acc[...] = jnp.zeros_like(log_acc)

    @pl.when(slot < count_ref[0])
    def _():
        src_at = pl.ds(pl.multiple_of(src_id[slot] * BLOCK, BLOCK), BLOCK)
        dst_at = pl.ds(pl.multiple_of(dst_id[slot] * BLOCK, BLOCK), BLOCK)
        dst_block = dst_ref[dst_at, :]
        prods = None
        part = 128
        for lo in range(0, BLOCK, part):
            rows = pl.ds(pl.multiple_of(src_id[slot] * BLOCK + lo, part), part)
            raw = dot_nt(src_ref[rows, :], dst_block)
            sign = jnp.where(mask_ref[0, lo:lo + part, :] == 0, 1.0, -1.0)
            half = jnp.tanh(raw * half_scale)
            grad_buf[lo:lo + part, :] = (half + sign).astype(BF16)
            hinge_acc[...] += halve(jnp.maximum(raw * sign, 0.0), jnp.add, 8)
            prod = halve(1.0 + jnp.abs(half), jnp.multiply, 8)
            prods = prod if prods is None else prods * prod
        log_acc[...] += (BLOCK // 8) * math.log(2.0) - jnp.log(prods)
        grad = grad_buf[...]
        src_acc[src_at, :] += jnp.dot(grad, dst_block, preferred_element_type=F32)
        dst_acc[dst_at, :] += dot_tn(grad, src_ref[src_at, :])

    @pl.when(slot == pl.num_programs(0) - 1)
    def _():
        src_out[...] = src_acc[...].astype(BF16)
        dst_out[...] = dst_acc[...].astype(BF16)
        total = hinge_acc[...] * (2.0 * half_scale) + log_acc[...]
        loss_out[...] = jnp.broadcast_to(jnp.sum(total, keepdims=True), loss_out.shape)


def tiles(src_rows, dst_rows, tile_src, tile_dst, tile_mask, tile_count):
    slots = tile_mask.shape[0]
    width = src_rows.shape[1]
    whole = lambda j, *_: (0, 0)
    return pl.pallas_call(
        functools.partial(tile_kernel, 0.5 * width ** -0.5),
        out_shape=(
            jax.ShapeDtypeStruct(src_rows.shape, BF16),
            jax.ShapeDtypeStruct(dst_rows.shape, BF16),
            jax.ShapeDtypeStruct((8, 128), F32),
        ),
        grid_spec=pltpu.PrefetchScalarGridSpec(
            num_scalar_prefetch=3,
            grid=(slots,),
            in_specs=[
                pl.BlockSpec(src_rows.shape, whole, pipeline_mode=pl.Buffered(1)),
                pl.BlockSpec(dst_rows.shape, whole, pipeline_mode=pl.Buffered(1)),
                pl.BlockSpec((1, BLOCK, BLOCK), lambda j, n, s, d: (jnp.minimum(j, n[0] - 1), 0, 0)),
            ],
            out_specs=[
                pl.BlockSpec(src_rows.shape, whole, pipeline_mode=pl.Buffered(1)),
                pl.BlockSpec(dst_rows.shape, whole, pipeline_mode=pl.Buffered(1)),
                pl.BlockSpec((8, 128), whole),
            ],
            scratch_shapes=[
                pltpu.VMEM(src_rows.shape, F32),
                pltpu.VMEM(dst_rows.shape, F32),
                pltpu.VMEM((BLOCK, BLOCK), BF16),
                pltpu.VMEM((8, BLOCK), F32),
                pltpu.VMEM((8, BLOCK), F32),
            ],
        ),
        compiler_params=pltpu.CompilerParams(vmem_limit_bytes=48 << 20),
        name="tiles",
    )(tile_count, tile_src, tile_dst, src_rows, dst_rows, tile_mask)


def advance(steps):
    return [step for step in steps if next(step, True) is None]


def together(*steps):
    steps = advance(steps)
    while steps:
        yield
        steps = advance(steps)


def finish(*steps):
    for _ in together(*steps):
        pass


def wavefront(steps):
    waiting = advance(steps)
    running = []
    while waiting or running:
        running = advance(waiting[:1] + running)
        waiting = waiting[1:]


def group(axis, n, inner):
    me = lax.axis_index(axis)
    return me, me // inner, lax.rem(me, inner)


def gather(axis, n, inner, src, place, send, recv):
    outer = n // inner
    me, at_o, at_i = group(axis, n, inner)

    def line(way, k):
        block = at_o - k if way == 0 else at_o + k
        ahead = me + inner if way == 0 else me - inner
        index = way * (outer - 1) + k
        return pltpu.make_async_remote_copy(
            src_ref=src if k == 0 else place(block * inner + at_i),
            dst_ref=place(me if k == 0 else block * inner + at_i),
            send_sem=send.at[index],
            recv_sem=recv.at[index],
            device_id={axis: ahead},
        )

    def sends(way, k):
        if way == 0:
            return jnp.logical_and(at_o - k >= 0, at_o < outer - 1)
        return jnp.logical_and(at_o + k < outer, at_o > 0)

    def arrived(way, k):
        block = at_o - 1 - k if way == 0 else at_o + 1 + k
        index = way * (outer - 1) + k
        here = place(block * inner + at_i)
        return pltpu.make_async_remote_copy(
            src_ref=here, dst_ref=here, send_sem=send.at[index], recv_sem=recv.at[index], device_id={axis: me}
        )

    def arrives(way, k):
        return at_o - 1 - k >= 0 if way == 0 else at_o + 1 + k < outer

    def across(j, block, slot, own, incoming=False):
        index = 2 * (outer - 1) + (j - 1) * (2 * outer - 1) + slot
        peer = at_o * inner + lax.rem(at_i + j, inner)
        where = place(block * inner + (lax.rem(at_i + inner - j, inner) if incoming else at_i))
        return pltpu.make_async_remote_copy(
            src_ref=src if own else where,
            dst_ref=where,
            send_sem=send.at[index],
            recv_sem=recv.at[index],
            device_id={axis: peer},
        )

    def slots():
        for way in range(2):
            for k in range(outer - 1):
                yield way, k, (at_o - 1 - k if way == 0 else at_o + 1 + k), 1 + way * (outer - 1) + k

    for way in range(2):
        @pl.when(sends(way, 0))
        def _(way=way):
            line(way, 0).start()
    for j in range(1, inner):
        across(j, at_o, 0, True).start()
    here = place(me)
    here[...] = src[...]
    yield
    for step in range(outer - 1):
        for way, k, block, slot in slots():
            if k != step:
                continue

            @pl.when(arrives(way, k))
            def _(way=way, k=k, block=block, slot=slot):
                arrived(way, k).wait_recv()
                for j in range(1, inner):
                    across(j, block, slot, False).start()
                if k + 1 < outer - 1:
                    @pl.when(sends(way, k + 1))
                    def _():
                        line(way, k + 1).start()
        yield
    for j in range(1, inner):
        across(j, at_o, 0, True, True).wait_recv()
        across(j, at_o, 0, True).wait_send()
    for way, k, block, slot in slots():
        @pl.when(arrives(way, k))
        def _(block=block, slot=slot):
            for j in range(1, inner):
                across(j, block, slot, False, True).wait_recv()
                across(j, block, slot, False).wait_send()

        @pl.when(sends(way, k))
        def _(way=way, k=k):
            line(way, k).wait_send()


def gather_sems(n, inner):
    outer = n // inner
    count = 2 * (outer - 1) + (inner - 1) * (2 * outer - 1)
    return [pltpu.SemaphoreType.DMA((count,)), pltpu.SemaphoreType.DMA((count,))]


def reduce(axis, n, inner, place, near, out, far, send, recv, result):
    outer = n // inner
    me, at_o, at_i = group(axis, n, inner)
    order = sorted(range(outer), key=lambda off: -min(off, outer - off))

    def across(j, off):
        index = (j - 1) * outer + off
        block = lax.rem(at_o + off, outer) * inner + lax.rem(at_i + j, inner)
        return pltpu.make_async_remote_copy(
            src_ref=place(block),
            dst_ref=near.at[index],
            send_sem=send.at[index],
            recv_sem=recv.at[index],
            device_id={axis: at_o * inner + lax.rem(at_i + j, inner)},
        )

    def along(off):
        index = (inner - 1) * outer + off - 1
        return pltpu.make_async_remote_copy(
            src_ref=out.at[off - 1],
            dst_ref=far.at[off - 1],
            send_sem=send.at[index],
            recv_sem=recv.at[index],
            device_id={axis: lax.rem(at_o + off, outer) * inner + at_i},
        )

    for off in order:
        for j in range(1, inner):
            across(j, off).start()
    yield
    for off in order:
        total = place(lax.rem(at_o + off, outer) * inner + at_i)[...].astype(F32)
        for j in range(1, inner):
            across(j, off).wait_recv()
            total = total + near[(j - 1) * outer + off].astype(F32)
        if off:
            out[off - 1] = total.astype(BF16)
            along(off).start()
    yield
    for off in order[:-1]:
        along(off).wait_recv()
        total = total + far[off - 1].astype(F32)
    result.append(total)
    for off in order:
        for j in range(1, inner):
            across(j, off).wait_send()
        if off:
            along(off).wait_send()


def reduce_scratch(n, inner, block):
    outer = n // inner
    count = (inner - 1) * outer + outer - 1
    return [
        pltpu.VMEM(((inner - 1) * outer,) + block, BF16),
        pltpu.VMEM((outer - 1,) + block, BF16),
        pltpu.VMEM((outer - 1,) + block, BF16),
        pltpu.SemaphoreType.DMA((count,)),
        pltpu.SemaphoreType.DMA((count,)),
    ]


def sum_over(axis, n, src, slots, send, recv, result):
    me = lax.axis_index(axis)

    def copy(j):
        return pltpu.make_async_remote_copy(
            src_ref=src,
            dst_ref=slots.at[j - 1],
            send_sem=send.at[j - 1],
            recv_sem=recv.at[j - 1],
            device_id={axis: lax.rem(me + j, n)},
        )

    for j in range(1, n):
        copy(j).start()
    yield
    total = src[...]
    for j in range(1, n):
        copy(j).wait_recv()
        total = total + slots[j - 1]
    result.append(total)
    for j in range(1, n):
        copy(j).wait_send()


def sum_scratch(n):
    return [
        pltpu.VMEM((n - 1, 8, 128), F32),
        pltpu.SemaphoreType.DMA((n - 1,)),
        pltpu.SemaphoreType.DMA((n - 1,)),
    ]


def greet(axes):
    barrier = pltpu.get_barrier_semaphore()
    total = 0
    for axis, n in axes:
        me = lax.axis_index(axis)
        for j in range(1, n):
            pl.semaphore_signal(barrier, inc=1, device_id={axis: lax.rem(me + j, n)})
        total += n - 1
    pl.semaphore_wait(barrier, total)


def rows_of(ref, size, part, chunk):
    return lambda block: ref.at[pl.ds(pl.multiple_of(block * size + chunk * part, part), part), :]


def units_of(ref, size, kind):
    return lambda block: ref.at[kind, pl.ds(pl.multiple_of(block * size, size), size), :]


def rows(ref, part, chunk):
    return ref.at[pl.ds(chunk * part, part), :]


def take(scratch, count):
    taken = scratch[:count]
    del scratch[:count]
    return taken


def gather_in_kernel(row, col, w_ref, x_ref, w_out, x_out, *scratch):
    greet((("row", row[0]), ("col", col[0])))
    scratch = list(scratch)
    kinds, units = w_ref.shape[:2]
    size = x_ref.shape[0]
    steps = [
        gather("col", *col, w_ref.at[kind], units_of(w_out, units, kind), *take(scratch, 2)) for kind in range(kinds)
    ]
    steps.append(gather("row", *row, x_ref, rows_of(x_out, size, size, 0), *take(scratch, 2)))
    finish(*steps)


def embed_kernel(row, col, chunks, branch_ref, x_ref, src_out, dst_out, held, *scratch):
    greet((("row", row[0]), ("col", col[0])))
    scratch = list(scratch)
    size = x_ref.shape[0]
    part = size // chunks

    def chain(chunk, sum_refs, col_sems, row_sems):
        branch = []
        yield from reduce("row", *row, rows_of(branch_ref, size, part, chunk), *sum_refs, branch)
        own = rows(held, part, chunk)
        own[...] = (rows(x_ref, part, chunk)[...].astype(F32) + branch[0]).astype(BF16)
        yield from together(
            gather("col", *col, own, rows_of(src_out, size, part, chunk), *col_sems),
            gather("row", *row, own, rows_of(dst_out, size, part, chunk), *row_sems),
        )

    wavefront([chain(chunk, take(scratch, 5), take(scratch, 2), take(scratch, 2)) for chunk in range(chunks)])


def grad_kernel(row, col, chunks, src_ref, dst_ref, tot_ref, grad_out, tot_out, held, tot_held, *scratch):
    greet((("row", row[0]), ("col", col[0])))
    scratch = list(scratch)
    size = held.shape[0]
    part = size // chunks

    def totals(row_refs, col_refs):
        first, second = [], []
        yield from sum_over("row", row[0], tot_ref, *row_refs, first)
        tot_held[...] = first[0]
        yield
        yield from sum_over("col", col[0], tot_held, *col_refs, second)
        tot_out[...] = second[0]

    def chain(chunk, col_refs, row_refs, row_sems):
        total = []
        yield from together(
            reduce("row", *row, rows_of(dst_ref, size, part, chunk), *row_refs, total),
            reduce("col", *col, rows_of(src_ref, size, part, chunk), *col_refs, total),
        )
        own = rows(held, part, chunk)
        own[...] = (total[0] + total[1]).astype(BF16)
        yield from gather("row", *row, own, rows_of(grad_out, size, part, chunk), *row_sems)

    steps = [totals(take(scratch, 3), take(scratch, 3))]
    steps += [chain(chunk, take(scratch, 5), take(scratch, 5), take(scratch, 2)) for chunk in range(chunks)]
    wavefront(steps)


def weight_kernel(col, part_ref, sum_out, *scratch):
    greet((("col", col[0]),))
    scratch = list(scratch)
    kinds, units = sum_out.shape[:2]

    def chain(kind, refs):
        total = []
        yield from reduce("col", *col, units_of(part_ref, units, kind), *refs, total)
        sum_out[kind] = total[0]

    wavefront([chain(kind, take(scratch, 5)) for kind in range(kinds)])


def remote(kernel, name, number, outs, scratch):
    vmem = pl.BlockSpec(memory_space=pltpu.VMEM)
    return pl.pallas_call(
        kernel,
        out_shape=outs,
        out_specs=jax.tree.map(lambda _: vmem, outs),
        scratch_shapes=scratch,
        compiler_params=pltpu.CompilerParams(
            collective_id=number, has_side_effects=True, vmem_limit_bytes=32 << 20
        ),
        name=name,
    )


def per_device(row, col, node_feats, w_gate, w_up, w_down, tile_src, tile_dst, tile_mask, tile_count):
    size, width = node_feats.shape
    units = w_down.shape[0]
    shaped = jax.ShapeDtypeStruct
    src_shape = shaped((col[0] * size, width), BF16)
    dst_shape = shaped((row[0] * size, width), BF16)
    stacked = jnp.stack((w_gate.T, w_up.T, w_down))
    weights, feats = remote(
        functools.partial(gather_in_kernel, row, col),
        "gather_in",
        0,
        (shaped((3, col[0] * units, width), BF16), dst_shape),
        gather_sems(*col) * 3 + gather_sems(*row),
    )(stacked, node_feats)
    gate_proj = dot_nt(feats, weights[0])
    up_proj = dot_nt(feats, weights[1])
    hidden = (jax.nn.silu(gate_proj) * up_proj).astype(BF16)
    branch = jnp.dot(hidden, weights[2], preferred_element_type=F32).astype(BF16)
    src_rows, dst_rows = remote(
        functools.partial(embed_kernel, row, col, CHUNKS),
        "embed",
        1,
        (src_shape, dst_shape),
        [pltpu.VMEM((size, width), BF16)]
        + (reduce_scratch(*row, (size // CHUNKS, width)) + gather_sems(*col) + gather_sems(*row)) * CHUNKS,
    )(branch, node_feats)
    src_part, dst_part, loss_part = tiles(src_rows, dst_rows, tile_src, tile_dst, tile_mask, tile_count)
    is_loss = lax.broadcasted_iota(jnp.int32, loss_part.shape, 0) == 0
    embed_grad, totals = remote(
        functools.partial(grad_kernel, row, col, CHUNKS),
        "grad",
        2,
        (dst_shape, shaped(loss_part.shape, F32)),
        [pltpu.VMEM((size, width), BF16), pltpu.VMEM(loss_part.shape, F32)]
        + sum_scratch(row[0]) + sum_scratch(col[0])
        + (
            reduce_scratch(*col, (size // CHUNKS, width))
            + reduce_scratch(*row, (size // CHUNKS, width))
            + gather_sems(*row)
        ) * CHUNKS,
    )(src_part, dst_part, jnp.where(is_loss, loss_part, tile_count[0].astype(F32)))
    hidden_grad = dot_nt(embed_grad, weights[2])
    sig = jax.nn.sigmoid(gate_proj)
    gate_grad = (hidden_grad * up_proj * sig * (1.0 + gate_proj * (1.0 - sig))).astype(BF16)
    up_grad = (hidden_grad * gate_proj * sig).astype(BF16)
    partial = jnp.stack(
        (dot_tn(gate_grad, feats).astype(BF16), dot_tn(up_grad, feats).astype(BF16), dot_tn(hidden, embed_grad).astype(BF16))
    )
    summed = remote(
        functools.partial(weight_kernel, col),
        "weight",
        3,
        shaped((3, units, width), F32),
        reduce_scratch(*col, (units, width)) * 3,
    )(partial)
    summed = summed * (0.5 * width ** -0.5 / totals[1, 0])
    entry_loss = totals[0, 0] / (totals[1, 0] * BLOCK * BLOCK)
    return (entry_loss, summed[0].T, summed[1].T, summed[2])


def solution(mesh):
    both = ("row", "col")
    in_specs = (
        P(both, None),
        P(None, both),
        P(None, both),
        P(both, None),
        P(both),
        P(both),
        P(both, None, None),
        P(both),
    )
    out_specs = (P(), P(None, both), P(None, both), P(both, None))
    row = (mesh.shape["row"], 2)
    col = (mesh.shape["col"], mesh.shape["col"] // 4)
    return jax.shard_map(functools.partial(per_device, row, col), mesh=mesh, in_specs=in_specs, out_specs=out_specs, check_vma=False)
```

profile of v0, /device:TPU:0, one launch (start us, length us, event | category | flops | bytes accessed | tf_op | source)
XLA Modules:
  0.0 167.2 jit_solution(3357140136829163368)
XLA Ops:
  0.6 0.9 pad_maximum_fusion.1.w_ref
  1.6 0.0 copy-start.1
  1.6 0.9 copy-done.1
  2.5 24.6 %gather_in.1 = (bf16[3,512,512]{2,1,0:T(8,128)(2,1)S(1)}, bf16[1024,512]{1,0:T(8,128)(2,1)S(1)}) custom-call(bf16[3,64,512]{2,1,0:T(8,128)(2,1)S(1)} %pad_maximum_fusion.1.w_ref, bf16[256,512]{1,0:T(8,128)(2,1)S(1)} %copy-done.1), custom_call_target="tpu_custom_call" | custom-call | tf_op jit(solution)/shard_map/gather_in/pallas_call | solution.py:452
  27.1 0.7 fusion.8
  27.9 1.0 multiply_convert_fusion.2
  28.9 0.0 copy-start.2
  28.9 0.0 copy-start.3
  28.9 0.0 copy-start.4
  28.9 0.7 convolution_convert_fusion.branch_ref
  29.6 0.2 copy-done.2
  29.8 33.6 %embed.1 = (bf16[2048,512]{1,0:T(8,128)(2,1)S(1)}, bf16[1024,512]{1,0:T(8,128)(2,1)S(1)}) custom-call(bf16[1024,512]{1,0:T(8,128)(2,1)S(1)} %convolution_convert_fusion.branch_ref, bf16[256,512]{1,0:T(8,128)(2,1)S(1)} %copy-done.2), custom_call_target="tpu_custom_call" | custom-call | tf_op jit(solution)/shard_map/embed/pallas_call | solution.py:463
  63.4 0.0 copy-start
  63.5 1.3 copy-done
  65.4 0.0 copy-done.3
  65.4 0.0 copy-done.4
  65.4 26.8 %tiles.1 = (bf16[2048,512]{1,0:T(8,128)(2,1)S(1)}, bf16[1024,512]{1,0:T(8,128)(2,1)S(1)}, f32[8,128]{1,0:T(8,128)S(1)}) custom-call(s32[1]{0:T(128)S(6)} %copy.12.count_ref, s32[16]{0:T(128)S(1)} %copy-done.3, s32[16]{0:T(128)S(1)} %copy-done.4, bf16[2048,512]{1,0:T(8,128)(2,1)} %copy-done, bf16[1024,512]{1,0:T(8,128)(2,1)S(1)} %get-tuple-element.16.dst_ref, ...), custom_call_target="tpu_custom_call" | custom-call | tf_op jit(solution)/shard_map/tiles/pallas_call | solution.py:79
  92.2 0.1 broadcast_select_fusion.tot_ref
  92.3 40.6 %grad.1 = (bf16[1024,512]{1,0:T(8,128)(2,1)S(1)}, f32[8,128]{1,0:T(8,128)S(1)}) custom-call(bf16[2048,512]{1,0:T(8,128)(2,1)S(1)} %get-tuple-element.17.src_ref, bf16[1024,512]{1,0:T(8,128)(2,1)S(1)} %get-tuple-element.18.dst_ref, f32[8,128]{1,0:T(8,128)S(1)} %broadcast_select_fusion.tot_ref), custom_call_target="tpu_custom_call" | custom-call | tf_op jit(solution)/shard_map/grad/pallas_call | solution.py:473
  133.0 0.7 fusion.3
  133.7 1.3 fusion
  135.0 0.8 fusion.1
  135.9 0.7 fusion.2
  136.6 0.2 pad_maximum_fusion.part_ref
  136.8 26.0 %weight.1 = f32[3,64,512]{2,1,0:T(8,128)S(1)} custom-call(bf16[3,512,512]{2,1,0:T(8,128)(2,1)S(1)} %pad_maximum_fusion.part_ref), custom_call_target="tpu_custom_call" | custom-call | tf_op jit(solution)/shard_map/weight/pallas_call | solution.py:493
  162.8 0.6 fusion.16
  164.1 0.8 slice_bitcast_fusion
  (2 shorter events, 0.0 us)
Async XLA Ops:
  1.6 1.0 copy-start.1
  28.9 1.0 copy-start.2
  28.9 36.6 %copy-start.3 = (s32[16]{0:T(128)S(1)}, s32[16]{0:T(128)}, u32[]{:S(2)}) copy-start(s32[16]{0:T(128)} %src_id.1) | copy-start | bytes 196
  28.9 36.6 %copy-start.4 = (s32[16]{0:T(128)S(1)}, s32[16]{0:T(128)}, u32[]{:S(2)}) copy-start(s32[16]{0:T(128)} %dst_id.1) | copy-start | bytes 196
  63.4 1.3 copy-start
where the time goes:
time: 167 us
  Pallas kernels  152 us (91%)
  matrix products  6.05 us (4%)
  between operations  4.55 us (3%)
  local copies, waits for them, and re-layouts  3.82 us (2%)
    pallas_call x1, Pallas kernels, per_device(): remote(functools.partial(grad_kernel, row, col, CHUNKS), 'grad', 2, (dst_...  40.6 us
    pallas_call x1, Pallas kernels, per_device(): remote(functools.partial(embed_kernel, row, col, CHUNKS), 'embed', 1, (sr...  33.6 us
    pallas_call x1, Pallas kernels, tiles(): pl.pallas_call(functools.partial(tile_kernel, 0.5 * width ** (-0.5)), out...  26.8 us
    pallas_call x1, Pallas kernels, per_device(): remote(functools.partial(weight_kernel, col), 'weight', 3, shaped((3, uni...  26 us
    pallas_call x1, Pallas kernels, per_device(): remote(functools.partial(gather_in_kernel, row, col), 'gather_in', 0, (sh...  24.6 us

commit v1 on v0

v1 whole, which is shorter than its diff:
```python
import functools
import math

import jax
import jax.numpy as jnp
from jax import lax
from jax.experimental import pallas as pl
from jax.experimental.pallas import tpu as pltpu
from jax.sharding import PartitionSpec as P

BLOCK = 512
NEAR, WIDE = 0, 1
SPLIT = ((4, NEAR), (4, NEAR), (3, NEAR), (2, NEAR), (3, WIDE))
F32 = jnp.float32
BF16 = jnp.bfloat16
NT = (((1,), (1,)), ((), ()))
TN = (((0,), (0,)), ((), ()))


def dot_nt(a, b):
    return lax.dot_general(a, b, NT, preferred_element_type=F32)


def dot_tn(a, b):
    return lax.dot_general(a, b, TN, preferred_element_type=F32)


def halve(x, op, rows):
    while x.shape[0] > rows:
        half = x.shape[0] // 2
        x = op(x[:half], x[half:])
    return x


def tile_kernel(half_scale, count_ref, src_id, dst_id, src_ref, dst_ref, mask_ref,
                src_out, dst_out, loss_out, src_acc, dst_acc, grad_buf, hinge_acc, log_acc):
    slot = pl.program_id(0)
    width = src_ref.shape[1]

    @pl.when(slot == 0)
    def _():
        src_acc[...] = jnp.zeros_like(src_acc)
        dst_acc[...] = jnp.zeros_like(dst_acc)
        hinge_acc[...] = jnp.zeros_like(hinge_acc)
        log_acc[...] = jnp.zeros_like(log_acc)

    @pl.when(slot < count_ref[0])
    def _():
        src_at = pl.ds(pl.multiple_of(src_id[slot] * BLOCK, BLOCK), BLOCK)
        dst_at = pl.ds(pl.multiple_of(dst_id[slot] * BLOCK, BLOCK), BLOCK)
        dst_block = dst_ref[dst_at, :]
        prods = None
        part = 128
        for lo in range(0, BLOCK, part):
            rows = pl.ds(pl.multiple_of(src_id[slot] * BLOCK + lo, part), part)
            raw = dot_nt(src_ref[rows, :], dst_block)
            sign = jnp.where(mask_ref[0, lo:lo + part, :] == 0, 1.0, -1.0)
            half = jnp.tanh(raw * half_scale)
            grad_buf[lo:lo + part, :] = (half + sign).astype(BF16)
            hinge_acc[...] += halve(jnp.maximum(raw * sign, 0.0), jnp.add, 8)
            prod = halve(1.0 + jnp.abs(half), jnp.multiply, 8)
            prods = prod if prods is None else prods * prod
        log_acc[...] += (BLOCK // 8) * math.log(2.0) - jnp.log(prods)
        grad = grad_buf[...]
        src_acc[src_at, :] += jnp.dot(grad, dst_block, preferred_element_type=F32)
        dst_acc[dst_at, :] += dot_tn(grad, src_ref[src_at, :])

    @pl.when(slot == pl.num_programs(0) - 1)
    def _():
        src_out[...] = src_acc[...].astype(BF16)
        dst_out[...] = dst_acc[...].astype(BF16)
        total = hinge_acc[...] * (2.0 * half_scale) + log_acc[...]
        is_loss = lax.broadcasted_iota(jnp.int32, loss_out.shape, 0) == 0
        loss_out[...] = jnp.where(is_loss, jnp.sum(total, keepdims=True), count_ref[0].astype(F32))


def tiles(src_rows, dst_rows, tile_src, tile_dst, tile_mask, tile_count):
    slots = tile_mask.shape[0]
    width = src_rows.shape[1]
    whole = lambda j, *_: (0, 0)
    return pl.pallas_call(
        functools.partial(tile_kernel, 0.5 * width ** -0.5),
        out_shape=(
            jax.ShapeDtypeStruct(src_rows.shape, BF16),
            jax.ShapeDtypeStruct(dst_rows.shape, BF16),
            jax.ShapeDtypeStruct((8, 128), F32),
        ),
        grid_spec=pltpu.PrefetchScalarGridSpec(
            num_scalar_prefetch=3,
            grid=(slots,),
            in_specs=[
                pl.BlockSpec(src_rows.shape, whole, pipeline_mode=pl.Buffered(1)),
                pl.BlockSpec(dst_rows.shape, whole, pipeline_mode=pl.Buffered(1)),
                pl.BlockSpec((1, BLOCK, BLOCK), lambda j, n, s, d: (jnp.minimum(j, n[0] - 1), 0, 0)),
            ],
            out_specs=[
                pl.BlockSpec(src_rows.shape, whole, pipeline_mode=pl.Buffered(1)),
                pl.BlockSpec(dst_rows.shape, whole, pipeline_mode=pl.Buffered(1)),
                pl.BlockSpec((8, 128), whole),
            ],
            scratch_shapes=[
                pltpu.VMEM(src_rows.shape, F32),
                pltpu.VMEM(dst_rows.shape, F32),
                pltpu.VMEM((BLOCK, BLOCK), BF16),
                pltpu.VMEM((8, BLOCK), F32),
                pltpu.VMEM((8, BLOCK), F32),
            ],
        ),
        compiler_params=pltpu.CompilerParams(vmem_limit_bytes=40 << 20),
        name="tiles",
    )(tile_count, tile_src, tile_dst, src_rows, dst_rows, tile_mask)


def advance(steps):
    return [step for step in steps if next(step, True) is None]


def together(*steps):
    steps = advance(steps)
    while steps:
        yield
        steps = advance(steps)


def finish(*steps):
    for _ in together(*steps):
        pass


def group(axis, n, inner):
    me = lax.axis_index(axis)
    return me, me // inner, lax.rem(me, inner)


def gather_near(axis, n, inner, src, place, send, recv):
    outer = n // inner
    me, at_o, at_i = group(axis, n, inner)

    def line(way, k):
        block = at_o - k if way == 0 else at_o + k
        ahead = me + inner if way == 0 else me - inner
        index = way * (outer - 1) + k
        return pltpu.make_async_remote_copy(
            src_ref=src if k == 0 else place(block * inner + at_i),
            dst_ref=place(me if k == 0 else block * inner + at_i),
            send_sem=send.at[index],
            recv_sem=recv.at[index],
            device_id={axis: ahead},
        )

    def sends(way, k):
        if way == 0:
            return jnp.logical_and(at_o - k >= 0, at_o < outer - 1)
        return jnp.logical_and(at_o + k < outer, at_o > 0)

    def arrived(way, k):
        block = at_o - 1 - k if way == 0 else at_o + 1 + k
        index = way * (outer - 1) + k
        here = place(block * inner + at_i)
        return pltpu.make_async_remote_copy(
            src_ref=here, dst_ref=here, send_sem=send.at[index], recv_sem=recv.at[index], device_id={axis: me}
        )

    def arrives(way, k):
        return at_o - 1 - k >= 0 if way == 0 else at_o + 1 + k < outer

    def across(j, block, slot, own, incoming=False):
        index = 2 * (outer - 1) + (j - 1) * (2 * outer - 1) + slot
        peer = at_o * inner + lax.rem(at_i + j, inner)
        where = place(block * inner + (lax.rem(at_i + inner - j, inner) if incoming else at_i))
        return pltpu.make_async_remote_copy(
            src_ref=src if own else where,
            dst_ref=where,
            send_sem=send.at[index],
            recv_sem=recv.at[index],
            device_id={axis: peer},
        )

    def slots():
        for way in range(2):
            for k in range(outer - 1):
                yield way, k, (at_o - 1 - k if way == 0 else at_o + 1 + k), 1 + way * (outer - 1) + k

    for way in range(2):
        @pl.when(sends(way, 0))
        def _(way=way):
            line(way, 0).start()
    for j in range(1, inner):
        across(j, at_o, 0, True).start()
    yield
    for step in range(outer - 1):
        for way, k, block, slot in slots():
            if k != step:
                continue

            @pl.when(arrives(way, k))
            def _(way=way, k=k, block=block, slot=slot):
                arrived(way, k).wait_recv()
                if k + 1 < outer - 1:
                    @pl.when(sends(way, k + 1))
                    def _():
                        line(way, k + 1).start()
                for j in range(1, inner):
                    across(j, block, slot, False).start()
        yield
    for j in range(1, inner):
        across(j, at_o, 0, True, True).wait_recv()
        across(j, at_o, 0, True).wait_send()
    for way, k, block, slot in slots():
        @pl.when(arrives(way, k))
        def _(block=block, slot=slot):
            for j in range(1, inner):
                across(j, block, slot, False, True).wait_recv()
                across(j, block, slot, False).wait_send()

        @pl.when(sends(way, k))
        def _(way=way, k=k):
            line(way, k).wait_send()


def gather_wide(axis, n, inner, src, place, send, recv):
    outer = n // inner
    me, at_o, at_i = group(axis, n, inner)

    def block(o, j):
        return o * inner + lax.rem(at_i + j, inner)

    def line(way, k, j, incoming=False):
        index = inner - 1 + (way * (outer - 1) + k) * inner + j
        step = k + 1 if incoming else k
        where = place(block(at_o - step if way == 0 else at_o + step, j))
        return pltpu.make_async_remote_copy(
            src_ref=src if k == 0 and j == 0 and not incoming else where,
            dst_ref=where,
            send_sem=send.at[index],
            recv_sem=recv.at[index],
            device_id={axis: me if incoming else me + inner if way == 0 else me - inner},
        )

    def sends(way, k):
        if way == 0:
            return jnp.logical_and(at_o - k >= 0, at_o < outer - 1)
        return jnp.logical_and(at_o + k < outer, at_o > 0)

    def arrives(way, k):
        return at_o - 1 - k >= 0 if way == 0 else at_o + 1 + k < outer

    def across(j, incoming=False):
        where = place(block(at_o, inner - j if incoming else 0))
        return pltpu.make_async_remote_copy(
            src_ref=where if incoming else src,
            dst_ref=where,
            send_sem=send.at[j - 1],
            recv_sem=recv.at[j - 1],
            device_id={axis: block(at_o, j)},
        )

    for j in range(1, inner):
        across(j).start()
    for way in range(2):
        @pl.when(sends(way, 0))
        def _(way=way):
            line(way, 0, 0).start()
    yield
    for j in range(1, inner):
        across(j, True).wait_recv()
        for way in range(2):
            @pl.when(sends(way, 0))
            def _(way=way, j=j):
                line(way, 0, inner - j).start()
    yield
    for k in range(outer - 1):
        for way in range(2):
            @pl.when(arrives(way, k))
            def _(way=way, k=k):
                for j in range(inner):
                    line(way, k, j, True).wait_recv()
                    if k + 1 < outer - 1:
                        @pl.when(sends(way, k + 1))
                        def _(j=j):
                            line(way, k + 1, j).start()
        yield
    for j in range(1, inner):
        across(j).wait_send()
    for way in range(2):
        for k in range(outer - 1):
            @pl.when(sends(way, k))
            def _(way=way, k=k):
                for j in range(inner):
                    line(way, k, j).wait_send()


def gather_sems(n, inner, route=NEAR):
    outer = n // inner
    count = inner - 1 + 2 * (outer - 1) * inner
    if route == NEAR:
        count = 2 * (outer - 1) + (inner - 1) * (2 * outer - 1)
    return [pltpu.SemaphoreType.DMA((count,)), pltpu.SemaphoreType.DMA((count,))]


def gather(route, *args):
    return (gather_near, gather_wide)[route](*args)


def chain_line(axis, n, inner):
    outer = n // inner
    me, at_o, at_i = group(axis, n, inner)

    def exists(way, k):
        return at_o + k < outer if way == 0 else at_o - k >= 0

    def fed(way):
        return at_o > 0 if way == 0 else at_o < outer - 1

    def starts(way):
        return at_o == 0 if way == 0 else at_o == outer - 1

    def block(way, k, j):
        return (at_o + k if way == 0 else at_o - k) * inner + lax.rem(at_i + j, inner)

    return exists, fed, starts, block, (me + inner, me - inner)


def reduce_near(axis, n, inner, place, acc, near, out, inn, send, recv):
    outer = n // inner
    exists, fed, starts, block, ahead = chain_line(axis, n, inner)
    base = (inner - 1) * 2 * outer

    def across(j, way, k):
        index = (j - 1) * 2 * outer + way * outer + k
        return pltpu.make_async_remote_copy(
            src_ref=place(block(way, k, j)),
            dst_ref=near.at[index],
            send_sem=send.at[index],
            recv_sem=recv.at[index],
            device_id={axis: block(0, 0, j)},
        )

    def along(way, k):
        slot = way * outer + k
        return pltpu.make_async_remote_copy(
            src_ref=out.at[slot],
            dst_ref=inn.at[slot - 1],
            send_sem=send.at[base + slot],
            recv_sem=recv.at[base + slot - 1],
            device_id={axis: ahead[way]},
        )

    def arrived(way, k):
        slot = way * outer + k
        return pltpu.make_async_remote_copy(
            src_ref=inn.at[slot],
            dst_ref=inn.at[slot],
            send_sem=send.at[base + slot],
            recv_sem=recv.at[base + slot],
            device_id={axis: block(0, 0, 0)},
        )

    def local(way, k):
        total = place(block(way, k, 0))[...].astype(F32)
        for j in range(1, inner):
            across(j, way, k).wait_recv()
            total = total + near[(j - 1) * 2 * outer + way * outer + k].astype(F32)
        return total

    hops = [(way, k) for k in range(outer - 1, 0, -1) for way in range(2)]
    for way, k in hops:
        @pl.when(exists(way, k))
        def _(way=way, k=k):
            for j in range(1, inner):
                across(j, way, k).start()
        if way == 1:
            yield
    for way, k in hops:
        @pl.when(exists(way, k))
        def _(way=way, k=k):
            slot = way * outer + k
            total = local(way, k)
            if k == outer - 1:
                out[slot] = total.astype(BF16)
            else:
                @pl.when(starts(way))
                def _():
                    out[slot] = total.astype(BF16)

                @pl.when(fed(way))
                def _():
                    arrived(way, k).wait_recv()
                    out[slot] = (total + inn[slot].astype(F32)).astype(BF16)
            along(way, k).start()
        if way == 1 and k == 1:
            for j in range(1, inner):
                across(j, 0, 0).start()
        if way == 1:
            yield
    acc[0] = local(0, 0)
    for way in range(2):
        @pl.when(fed(way))
        def _(way=way):
            arrived(way, 0).wait_recv()
            acc[0] += inn[way * outer].astype(F32)
    for j in range(1, inner):
        across(j, 0, 0).wait_send()
    for way, k in hops:
        @pl.when(exists(way, k))
        def _(way=way, k=k):
            for j in range(1, inner):
                across(j, way, k).wait_send()
            along(way, k).wait_send()


def reduce_wide(axis, n, inner, place, acc, near, out, inn, send, recv):
    outer = n // inner
    exists, fed, starts, block, ahead = chain_line(axis, n, inner)
    base = inner - 1

    def along(way, k, j, first):
        slot = (way * outer + k) * inner + j
        return pltpu.make_async_remote_copy(
            src_ref=place(block(way, k, j)) if first else out.at[slot],
            dst_ref=inn.at[slot - inner],
            send_sem=send.at[base + slot],
            recv_sem=recv.at[base + slot - inner],
            device_id={axis: ahead[way]},
        )

    def arrived(way, k, j):
        slot = (way * outer + k) * inner + j
        return pltpu.make_async_remote_copy(
            src_ref=inn.at[slot],
            dst_ref=inn.at[slot],
            send_sem=send.at[base + slot],
            recv_sem=recv.at[base + slot],
            device_id={axis: block(0, 0, 0)},
        )

    def across(j):
        return pltpu.make_async_remote_copy(
            src_ref=out.at[j],
            dst_ref=near.at[j - 1],
            send_sem=send.at[j - 1],
            recv_sem=recv.at[j - 1],
            device_id={axis: block(0, 0, j)},
        )

    hops = [(way, k) for k in range(outer - 1, 0, -1) for way in range(2)]
    for way, k in hops:
        @pl.when(jnp.logical_and(exists(way, k), starts(way)))
        def _(way=way, k=k):
            for j in range(inner):
                along(way, k, j, True).start()
    yield
    yield
    for way, k in hops:
        if k == outer - 1:
            continue

        @pl.when(jnp.logical_and(exists(way, k), fed(way)))
        def _(way=way, k=k):
            for j in range(inner):
                slot = (way * outer + k) * inner + j
                arrived(way, k, j).wait_recv()
                total = place(block(way, k, j))[...].astype(F32) + inn[slot].astype(F32)
                out[slot] = total.astype(BF16)
                along(way, k, j, False).start()
        if way == 1:
            yield
    for j in range(inner):
        acc[j] = place(block(0, 0, j))[...].astype(F32)
    for way in range(2):
        @pl.when(fed(way))
        def _(way=way):
            for j in range(inner):
                arrived(way, 0, j).wait_recv()
                acc[j] += inn[way * outer * inner + j].astype(F32)
    for j in range(1, inner):
        out[j] = acc[j].astype(BF16)
        across(j).start()
    yield
    for j in range(1, inner):
        across(j).wait_recv()
        acc[0] += near[j - 1].astype(F32)
        across(j).wait_send()
    for way, k in hops:
        for first, test in ((True, starts), (False, fed)):
            if k == outer - 1 and not first:
                continue

            @pl.when(jnp.logical_and(exists(way, k), test(way)))
            def _(way=way, k=k, first=first):
                for j in range(inner):
                    along(way, k, j, first).wait_send()


def reduce(route, *args):
    return (reduce_near, reduce_wide)[route](*args)


def reduce_scratch(n, inner, block, route=NEAR):
    outer = n // inner
    near, slots, sums = (inner - 1) * 2 * outer, 2 * outer, 1
    if route == WIDE:
        near, slots, sums = inner - 1, 2 * outer * inner, inner
    return [
        pltpu.VMEM((sums,) + block, F32),
        pltpu.VMEM((near,) + block, BF16),
        pltpu.VMEM((slots,) + block, BF16),
        pltpu.VMEM((slots,) + block, BF16),
        pltpu.SemaphoreType.DMA((near + slots,)),
        pltpu.SemaphoreType.DMA((near + slots,)),
    ]


def greet(axes):
    barrier = pltpu.get_barrier_semaphore()
    total = 0
    for axis, (n, inner) in axes:
        outer = n // inner
        me, at_o, at_i = group(axis, n, inner)
        for j in range(1, inner):
            pl.semaphore_signal(barrier, inc=1, device_id={axis: at_o * inner + lax.rem(at_i + j, inner)})

        @pl.when(at_o > 0)
        def _():
            pl.semaphore_signal(barrier, inc=1, device_id={axis: me - inner})

        @pl.when(at_o < outer - 1)
        def _():
            pl.semaphore_signal(barrier, inc=1, device_id={axis: me + inner})

        total += inner - 1 + lax.div(at_o + outer - 1, outer) + lax.div(2 * outer - 2 - at_o, outer)
    pl.semaphore_wait(barrier, total)


def spans(size):
    unit = size // sum(count for count, _ in SPLIT)
    at = 0
    for count, route in SPLIT:
        yield at, count * unit, route
        at += count * unit


def ahead(pieces):
    return sorted(pieces, key=lambda piece: -piece[2])


def rows_of(ref, size, at, part):
    return lambda block: ref.at[pl.ds(pl.multiple_of(block * size + at, math.gcd(size, at)), part), :]


def take(scratch, count):
    taken = scratch[:count]
    del scratch[:count]
    return taken


def pick(ref, size, at, part):
    return jnp.concatenate([ref[lo:lo + part, :] for lo in range(at, ref.shape[0], size)], axis=0)


def place_back(ref, size, at, part, value):
    for n, lo in enumerate(range(at, ref.shape[0], size)):
        ref[lo:lo + part, :] = value[n * part:(n + 1) * part, :]


def unit_spans(units):
    return ((0, 0, units, NEAR), (1, 0, units, NEAR), (2, 0, units // 2, WIDE), (2, units // 2, units // 2, NEAR))


def forward_kernel(row, col, gate_ref, up_ref, down_ref, x_ref, src_out, dst_out, feats, down_all, hidden,
                   gate_fac, up_fac, gate_all, up_all, branch, own_sem, *scratch):
    scratch = list(scratch)
    units, size = gate_ref.shape[0], x_ref.shape[0]
    whole = (gate_all, up_all, down_all)
    mine = (gate_ref, up_ref, down_ref)
    at_row, at_col = lax.axis_index("row"), lax.axis_index("col")
    local = [
        pltpu.make_async_copy(mine[kind], rows_of(whole[kind], units, 0, units)(at_col), own_sem.at[kind])
        for kind in range(3)
    ]
    local.append(pltpu.make_async_copy(x_ref, rows_of(feats, size, 0, size)(at_row), own_sem.at[3]))
    for copy in local:
        copy.start()
    greet((("row", row), ("col", col)))
    early, late = [], []
    for kind, at, part, route in unit_spans(units):
        src = mine[kind].at[pl.ds(at, part), :]
        steps = gather(route, "col", *col, src, rows_of(whole[kind], units, at, part), *take(scratch, 2))
        (late if kind == 2 else early).append(steps)
    early.append(gather(NEAR, "row", *row, x_ref, rows_of(feats, size, 0, size), *take(scratch, 2)))
    early, late = advance(early), advance(late)
    while early:
        early, late = advance(early), late and advance(late)
    for copy in local:
        copy.wait()

    @pl.loop(0, row[0])
    def _(n):
        at = pl.ds(pl.multiple_of(n * size, size), size)
        gate = dot_nt(feats[at, :], gate_all[...])
        up = dot_nt(feats[at, :], up_all[...])
        sig = jax.nn.sigmoid(gate)
        silu = gate * sig
        hidden[at, :] = (silu * up).astype(BF16)
        gate_fac[at, :] = up * sig * (1.0 + gate * (1.0 - sig))
        up_fac[at, :] = silu

    finish(*late)

    def chain(at, part, route, sums, col_sems, row_sems):
        value = jnp.dot(pick(hidden, size, at, part), down_all[...], preferred_element_type=F32)
        place_back(branch, size, at, part, value.astype(BF16))
        yield from reduce(NEAR, "row", *row, rows_of(branch, size, at, part), *sums)
        here = rows_of(src_out, size, at, part)(at_col)
        held = rows_of(dst_out, size, at, part)(at_row)
        value = (rows_of(feats, size, at, part)(at_row)[...].astype(F32) + sums[0][0]).astype(BF16)
        here[...] = value
        held[...] = value
        yield from together(
            gather(route, "col", *col, here, rows_of(src_out, size, at, part), *col_sems),
            gather(NEAR, "row", *row, held, rows_of(dst_out, size, at, part), *row_sems),
        )

    finish(*[
        chain(at, part, route, take(scratch, 6), take(scratch, 2), take(scratch, 2))
        for at, part, route in ahead(spans(size))
    ])


def backward_kernel(row, col, factor, src_ref, dst_ref, tot_ref, feats, down_all, hidden, gate_fac, up_fac,
                    loss_out, gate_out, up_out, down_out, grad_all, gate_grad, up_grad, parts, tot_row, tot_col,
                    *scratch):
    scratch = list(scratch)
    size, units = feats.shape[0] // row[0], down_out.shape[0]
    at_row, at_col = lax.axis_index("row"), lax.axis_index("col")
    greet((("row", row), ("col", col)))
    tot_row[at_row] = tot_ref[...]

    def totals(row_sems, col_sems):
        yield from gather(NEAR, "row", *row, tot_row.at[at_row], lambda block: tot_row.at[block], *row_sems)
        total = tot_row[0]
        for n in range(1, row[0]):
            total = total + tot_row[n]
        tot_col[at_col] = total
        yield
        yield from gather(NEAR, "col", *col, tot_col.at[at_col], lambda block: tot_col.at[block], *col_sems)

    def chain(at, part, route, col_refs, row_refs, row_sems):
        yield from together(
            reduce(NEAR, "row", *row, rows_of(dst_ref, size, at, part), *row_refs),
            reduce(route, "col", *col, rows_of(src_ref, size, at, part), *col_refs),
        )
        own = rows_of(grad_all, size, at, part)(at_row)
        own[...] = (row_refs[0][0] + col_refs[0][0]).astype(BF16)
        yield from gather(NEAR, "row", *row, own, rows_of(grad_all, size, at, part), *row_sems)
        hidden_grad = dot_nt(pick(grad_all, size, at, part), down_all[...])
        place_back(gate_grad, size, at, part, (hidden_grad * pick(gate_fac, size, at, part)).astype(BF16))
        place_back(up_grad, size, at, part, (hidden_grad * pick(up_fac, size, at, part)).astype(BF16))

    steps = [
        chain(at, part, route, take(scratch, 6), take(scratch, 6), take(scratch, 2)) for at, part, route in spans(size)
    ]
    steps.append(totals(take(scratch, 2), take(scratch, 2)))
    finish(*steps)

    outs = (gate_out, up_out, down_out)
    running = []
    total = tot_col[0]
    for n in range(1, col[0]):
        total = total + tot_col[n]
    scale = factor / total[1:2, :1]

    def spread(kind, at, part, route, refs):
        yield from reduce(route, "col", *col, rows_of(parts.at[kind], units, at, part), *refs)
        outs[kind][at:at + part, :] = refs[0][0] * scale

    for kind, left, right in ((2, hidden, grad_all), (1, up_grad, feats), (0, gate_grad, feats)):
        parts[kind] = dot_tn(left[...], right[...]).astype(BF16)
        for found, at, part, route in unit_spans(units):
            if found == kind:
                running.append(spread(kind, at, part, route, take(scratch, 6)))
                advance(running[-1:])
    loss_out[...] = jnp.broadcast_to(total[0:1, :] / (total[1:2, :] * BLOCK * BLOCK), loss_out.shape)
    finish(*running)


def per_device(row, col, node_feats, w_gate, w_up, w_down, tile_src, tile_dst, tile_mask, tile_count):
    size, width = node_feats.shape
    units = w_down.shape[0]
    shaped = jax.ShapeDtypeStruct
    vmem, hbm = pl.BlockSpec(memory_space=pltpu.VMEM), pl.BlockSpec(memory_space=pltpu.HBM)
    nodes, wide = row[0] * size, col[0] * units
    weight = pltpu.VMEM((wide, width), BF16)
    pieces = list(spans(size))
    scratch = [weight, weight, pltpu.VMEM((nodes, width), BF16), pltpu.SemaphoreType.DMA((4,))]
    for _, _, _, route in unit_spans(units):
        scratch += gather_sems(*col, route)
    scratch += gather_sems(*row)
    for _, part, route in ahead(pieces):
        scratch += reduce_scratch(*row, (part, width)) + gather_sems(*col, route) + gather_sems(*row)
    src_rows, dst_rows, *saved = pl.pallas_call(
        functools.partial(forward_kernel, row, col),
        out_shape=(
            shaped((col[0] * size, width), BF16),
            shaped((nodes, width), BF16),
            shaped((nodes, width), BF16),
            shaped((wide, width), BF16),
            shaped((nodes, wide), BF16),
            shaped((nodes, wide), F32),
            shaped((nodes, wide), F32),
        ),
        in_specs=[hbm] * 4,
        out_specs=(vmem,) * 7,
        scratch_shapes=scratch,
        compiler_params=pltpu.CompilerParams(collective_id=0, has_side_effects=True, vmem_limit_bytes=32 << 20),
        name="forward",
    )(w_gate.T, w_up.T, w_down, node_feats)
    src_part, dst_part, loss_part = tiles(src_rows, dst_rows, tile_src, tile_dst, tile_mask, tile_count)
    tots = loss_part.shape
    scratch = [pltpu.VMEM((nodes, width), BF16), pltpu.VMEM((nodes, wide), BF16), pltpu.VMEM((nodes, wide), BF16)]
    scratch += [pltpu.VMEM((3, wide, width), BF16), pltpu.VMEM((row[0],) + tots, F32), pltpu.VMEM((col[0],) + tots, F32)]
    for _, part, route in pieces:
        scratch += reduce_scratch(*col, (part, width), route) + reduce_scratch(*row, (part, width)) + gather_sems(*row)
    scratch += gather_sems(*row) + gather_sems(*col)
    for kind in (2, 1, 0):
        for found, _, part, route in unit_spans(units):
            if found == kind:
                scratch += reduce_scratch(*col, (part, width), route)
    loss, gate, up, down = pl.pallas_call(
        functools.partial(backward_kernel, row, col, 0.5 * width ** -0.5),
        out_shape=(shaped(tots, F32),) + (shaped((units, width), F32),) * 3,
        in_specs=[vmem] * 8,
        out_specs=(vmem,) * 4,
        scratch_shapes=scratch,
        compiler_params=pltpu.CompilerParams(collective_id=1, has_side_effects=True, vmem_limit_bytes=44 << 20),
        name="backward",
    )(src_part, dst_part, loss_part, *saved)
    return (loss[0, 0], gate.T, up.T, down)


def solution(mesh):
    both = ("row", "col")
    in_specs = (
        P(both, None),
        P(None, both),
        P(None, both),
        P(both, None),
        P(both),
        P(both),
        P(both, None, None),
        P(both),
    )
    out_specs = (P(), P(None, both), P(None, both), P(both, None))
    row = (mesh.shape["row"], 2)
    col = (mesh.shape["col"], mesh.shape["col"] // 4)
    return jax.shard_map(functools.partial(per_device, row, col), mesh=mesh, in_specs=in_specs, out_specs=out_specs, check_vma=False)
```

time: 167 us -> 146 us (0.87)
  Pallas kernels: 152 us -> 137 us
  matrix products: 6.05 us -> 0 us
  local copies, waits for them, and re-layouts: 3.82 us -> 7.24 us
  between operations: 4.55 us -> 1.33 us
    pallas_call x4 -> x2, Pallas kernels: 125 us -> 110 us  [the longest x1 55.1 us: per_device(): pl.pallas_call(functools.partial(forward_kernel, row, col), out_shape=(sh...]
    dot_general x7 -> x0, matrix products: 6.05 us -> none  [the longest x3 2.91 us: dot_tn(): return lax.dot_general(a, b, TN, preferred_element_type=F32)]
    unnamed x10 -> x15, local copies, waits for them, and re-layouts: 2.49 us -> 6.73 us
where the time goes in v1:
time: 146 us; the launch traced here: 145 us
  Pallas kernels  137 us (94%)
  local copies, waits for them, and re-layouts  7.24 us (5%)
    pallas_call x1, Pallas kernels, per_device(): pl.pallas_call(functools.partial(forward_kernel, row, col), out_shape=(sh...  55.1 us
    pallas_call x1, Pallas kernels, per_device(): pl.pallas_call(functools.partial(backward_kernel, row, col, 0.5 * width *...  55 us
    pallas_call x1, Pallas kernels, tiles(): pl.pallas_call(functools.partial(tile_kernel, 0.5 * width ** (-0.5)), out...  26.6 us
    unnamed x15, local copies, waits for them, and re-layouts  6.73 us

profile of v1, /device:TPU:0, one launch (start us, length us, event | category | flops | bytes accessed | tf_op | source)
XLA Modules:
  0.0 145.2 jit_solution(15756745726300006831)
XLA Ops:
  1.3 0.0 copy-start
  1.3 0.9 copy-done
  2.2 0.0 copy-start.1
  2.2 0.8 copy-done.1
  3.1 0.0 copy-start.2
  3.1 0.8 copy-done.2
  3.9 0.0 copy-start.3
  3.9 0.8 copy-done.3
  4.8 55.1 %forward.1 = (bf16[2048,512]{1,0:T(8,128)(2,1)S(1)}, bf16[1024,512]{1,0:T(8,128)(2,1)S(1)}, bf16[1024,512]{1,0:T(8,128)(2,1)S(1)}, bf16[512,512]{1,0:T(8,128)(2,...) custom-call(bf16[64,512]{1,0:T(8,128)(2,1)S(1)} %bitcast.7, ...), custom_call_target="tpu_custom_call" | custom-call | tf_op jit(solution)/shard_map/forward/pallas_call | solution.py:701
  59.9 0.0 copy-start.4
  59.9 0.6 copy-done.4
  60.5 0.0 copy-start.5
  60.5 0.7 copy-done.5
  61.2 26.6 %tiles.1 = (bf16[2048,512]{1,0:T(8,128)(2,1)S(1)}, bf16[1024,512]{1,0:T(8,128)(2,1)S(1)}, f32[8,128]{1,0:T(8,128)S(1)}) custom-call(s32[1]{0:T(128)S(6)} %copy.15.count_ref, s32[16]{0:T(128)S(1)} %copy-done.4, s32[16]{0:T(128)S(1)} %copy-done.5, bf16[2048,512]{1,0:T(8,128)(2,1)S(1)} %get-tuple-element.18.src_ref, ...), custom_call_target="tpu_custom_call" | custom-call | tf_op jit(solution)/shard_map/tiles/pallas_call | solution.py:81
  87.8 55.0 %backward.1 = (f32[8,128]{1,0:T(8,128)S(1)}, f32[64,512]{1,0:T(8,128)S(1)}, f32[64,512]{1,0:T(8,128)S(1)}, f32[64,512]{1,0:T(8,128)S(1)}) custom-call(bf16[2048,512]{1,0:T(8,128)(2,1)S(1)} %get-tuple-element.20.src_ref, bf16[1024,512]{1,0:T(8,128)(2,1)S(1)} %get-tuple-element.21.dst_ref, f32[8,128]{1,0:T(8,128)S(1)} %get-tuple-element.22.tot_ref, ...), custom_call_target="tpu_custom_call" | custom-call | tf_op jit(solution)/shard_map/backward/pallas_call | solution.py:729
  142.8 0.5 slice.3
  143.3 0.7 copy.16
  143.9 0.7 copy.17
  144.6 0.7 copy.18
Async XLA Ops:
  1.3 1.0 copy-start
  2.2 0.8 copy-start.1
  3.1 0.8 copy-start.2
  3.9 0.8 copy-start.3
  59.9 0.7 copy-start.4
  60.5 0.7 copy-start.5

commit v2 on v1

--- a/solution.py
+++ b/solution.py
@@ -32,7 +32,7 @@
     return x
 
 
-def tile_kernel(half_scale, count_ref, src_id, dst_id, src_ref, dst_ref, mask_ref,
+def tile_kernel(half_scale, count_ref, ids, src_ref, dst_ref, mask_ref,
                 src_out, dst_out, loss_out, src_acc, dst_acc, grad_buf, hinge_acc, log_acc):
     slot = pl.program_id(0)
     width = src_ref.shape[1]
@@ -46,13 +46,13 @@
 
     @pl.when(slot < count_ref[0])
     def _():
-        src_at = pl.ds(pl.multiple_of(src_id[slot] * BLOCK, BLOCK), BLOCK)
-        dst_at = pl.ds(pl.multiple_of(dst_id[slot] * BLOCK, BLOCK), BLOCK)
+        src_at = pl.ds(pl.multiple_of(ids[0, slot] * BLOCK, BLOCK), BLOCK)
+        dst_at = pl.ds(pl.multiple_of(ids[1, slot] * BLOCK, BLOCK), BLOCK)
         dst_block = dst_ref[dst_at, :]
         prods = None
         part = 128
         for lo in range(0, BLOCK, part):
-            rows = pl.ds(pl.multiple_of(src_id[slot] * BLOCK + lo, part), part)
+            rows = pl.ds(pl.multiple_of(ids[0, slot] * BLOCK + lo, part), part)
             raw = dot_nt(src_ref[rows, :], dst_block)
             sign = jnp.where(mask_ref[0, lo:lo + part, :] == 0, 1.0, -1.0)
             half = jnp.tanh(raw * half_scale)
@@ -86,12 +86,12 @@
             jax.ShapeDtypeStruct((8, 128), F32),
         ),
         grid_spec=pltpu.PrefetchScalarGridSpec(
-            num_scalar_prefetch=3,
+            num_scalar_prefetch=2,
             grid=(slots,),
             in_specs=[
                 pl.BlockSpec(src_rows.shape, whole, pipeline_mode=pl.Buffered(1)),
                 pl.BlockSpec(dst_rows.shape, whole, pipeline_mode=pl.Buffered(1)),
-                pl.BlockSpec((1, BLOCK, BLOCK), lambda j, n, s, d: (jnp.minimum(j, n[0] - 1), 0, 0)),
+                pl.BlockSpec((1, BLOCK, BLOCK), lambda j, n, s: (jnp.minimum(j, n[0] - 1), 0, 0)),
             ],
             out_specs=[
                 pl.BlockSpec(src_rows.shape, whole, pipeline_mode=pl.Buffered(1)),
@@ -108,7 +108,7 @@
         ),
         compiler_params=pltpu.CompilerParams(vmem_limit_bytes=40 << 20),
         name="tiles",
-    )(tile_count, tile_src, tile_dst, src_rows, dst_rows, tile_mask)
+    )(tile_count, jnp.stack((tile_src, tile_dst)), src_rows, dst_rows, tile_mask)
 
 
 def advance(steps):
@@ -143,7 +143,7 @@
         return pltpu.make_async_remote_copy(
             src_ref=src if k == 0 else place(block * inner + at_i),
             dst_ref=place(me if k == 0 else block * inner + at_i),
-            send_sem=send.at[index],
+            send_sem=send.at[0],
             recv_sem=recv.at[index],
             device_id={axis: ahead},
         )
@@ -158,64 +158,74 @@
         index = way * (outer - 1) + k
         here = place(block * inner + at_i)
         return pltpu.make_async_remote_copy(
-            src_ref=here, dst_ref=here, send_sem=send.at[index], recv_sem=recv.at[index], device_id={axis: me}
+            src_ref=here, dst_ref=here, send_sem=send.at[0], recv_sem=recv.at[index], device_id={axis: me}
         )
 
     def arrives(way, k):
         return at_o - 1 - k >= 0 if way == 0 else at_o + 1 + k < outer
 
-    def across(j, block, slot, own, incoming=False):
-        index = 2 * (outer - 1) + (j - 1) * (2 * outer - 1) + slot
-        peer = at_o * inner + lax.rem(at_i + j, inner)
-        where = place(block * inner + (lax.rem(at_i + inner - j, inner) if incoming else at_i))
+    def across(j, block, own):
+        where = place(block * inner + at_i)
         return pltpu.make_async_remote_copy(
             src_ref=src if own else where,
             dst_ref=where,
-            send_sem=send.at[index],
-            recv_sem=recv.at[index],
-            device_id={axis: peer},
+            send_sem=send.at[1],
+            recv_sem=recv.at[2 * (outer - 1)],
+            device_id={axis: at_o * inner + lax.rem(at_i + j, inner)},
+        )
+
+    def bulk(count, sent):
+        return pltpu.make_async_remote_copy(
+            src_ref=place.span(count),
+            dst_ref=place.span(count),
+            send_sem=send.at[sent],
+            recv_sem=recv.at[2 * (outer - 1)],
+            device_id={axis: me},
         )
 
     def slots():
         for way in range(2):
             for k in range(outer - 1):
-                yield way, k, (at_o - 1 - k if way == 0 else at_o + 1 + k), 1 + way * (outer - 1) + k
+                yield way, k, (at_o - 1 - k if way == 0 else at_o + 1 + k)
 
     for way in range(2):
         @pl.when(sends(way, 0))
         def _(way=way):
             line(way, 0).start()
     for j in range(1, inner):
-        across(j, at_o, 0, True).start()
+        across(j, at_o, True).start()
     yield
     for step in range(outer - 1):
-        for way, k, block, slot in slots():
+        for way, k, block in slots():
             if k != step:
                 continue
 
             @pl.when(arrives(way, k))
-            def _(way=way, k=k, block=block, slot=slot):
+            def _(way=way, k=k, block=block):
                 arrived(way, k).wait_recv()
                 if k + 1 < outer - 1:
                     @pl.when(sends(way, k + 1))
                     def _():
                         line(way, k + 1).start()
                 for j in range(1, inner):
-                    across(j, block, slot, False).start()
+                    across(j, block, False).start()
         yield
-    for j in range(1, inner):
-        across(j, at_o, 0, True, True).wait_recv()
-        across(j, at_o, 0, True).wait_send()
-    for way, k, block, slot in slots():
-        @pl.when(arrives(way, k))
-        def _(block=block, slot=slot):
-            for j in range(1, inner):
-                across(j, block, slot, False, True).wait_recv()
-                across(j, block, slot, False).wait_send()
-
-        @pl.when(sends(way, k))
-        def _(way=way, k=k):
-            line(way, k).wait_send()
+    bulk(outer * (inner - 1), 1).wait_recv()
+    bulk(outer * (inner - 1), 1).wait_send()
+    wait_line(outer, at_o, lambda count: bulk(count, 0).wait_send())
+
+
+def wait_line(outer, at_o, wait):
+    edge = jnp.logical_or(at_o == 0, at_o == outer - 1)
+
+    @pl.when(edge)
+    def _():
+        wait(1)
+
+    if outer > 2:
+        @pl.when(jnp.logical_not(edge))
+        def _():
+            wait(outer + 1)
 
 
 def gather_wide(axis, n, inner, src, place, send, recv):
@@ -232,7 +242,7 @@
         return pltpu.make_async_remote_copy(
             src_ref=src if k == 0 and j == 0 and not incoming else where,
             dst_ref=where,
-            send_sem=send.at[index],
+            send_sem=send.at[0],
             recv_sem=recv.at[index],
             device_id={axis: me if incoming else me + inner if way == 0 else me - inner},
         )
@@ -250,7 +260,7 @@
         return pltpu.make_async_remote_copy(
             src_ref=where if incoming else src,
             dst_ref=where,
-            send_sem=send.at[j - 1],
+            send_sem=send.at[1],
             recv_sem=recv.at[j - 1],
             device_id={axis: block(at_o, j)},
         )
@@ -280,22 +290,23 @@
                         def _(j=j):
                             line(way, k + 1, j).start()
         yield
-    for j in range(1, inner):
-        across(j).wait_send()
-    for way in range(2):
-        for k in range(outer - 1):
-            @pl.when(sends(way, k))
-            def _(way=way, k=k):
-                for j in range(inner):
-                    line(way, k, j).wait_send()
+    def sent(count, sem):
+        pltpu.make_async_remote_copy(
+            src_ref=place.span(count),
+            dst_ref=place.span(count),
+            send_sem=send.at[sem],
+            recv_sem=recv.at[0],
+            device_id={axis: me},
+        ).wait_send()
+
+    sent(inner - 1, 1)
+    wait_line(outer, at_o, lambda count: sent(count * inner, 0))
 
 
 def gather_sems(n, inner, route=NEAR):
     outer = n // inner
-    count = inner - 1 + 2 * (outer - 1) * inner
-    if route == NEAR:
-        count = 2 * (outer - 1) + (inner - 1) * (2 * outer - 1)
-    return [pltpu.SemaphoreType.DMA((count,)), pltpu.SemaphoreType.DMA((count,))]
+    count = 2 * (outer - 1) + 1 if route == NEAR else inner - 1 + 2 * (outer - 1) * inner
+    return [pltpu.SemaphoreType.DMA((2,)), pltpu.SemaphoreType.DMA((count,))]
 
 
 def gather(route, *args):
@@ -324,15 +335,15 @@
 def reduce_near(axis, n, inner, place, acc, near, out, inn, send, recv):
     outer = n // inner
     exists, fed, starts, block, ahead = chain_line(axis, n, inner)
-    base = (inner - 1) * 2 * outer
+    base = (inner - 1) * (2 * outer - 1)
 
     def across(j, way, k):
         index = (j - 1) * 2 * outer + way * outer + k
         return pltpu.make_async_remote_copy(
             src_ref=place(block(way, k, j)),
             dst_ref=near.at[index],
-            send_sem=send.at[index],
-            recv_sem=recv.at[index],
+            send_sem=send.at[0],
+            recv_sem=recv.at[(j - 1) * (2 * outer - 1) + way * (outer - 1) + k],
             device_id={axis: block(0, 0, j)},
         )
 
@@ -341,8 +352,8 @@
         return pltpu.make_async_remote_copy(
             src_ref=out.at[slot],
             dst_ref=inn.at[slot - 1],
-            send_sem=send.at[base + slot],
-            recv_sem=recv.at[base + slot - 1],
+            send_sem=send.at[0],
+            recv_sem=recv.at[base + way * (outer - 1) + k - 1],
             device_id={axis: ahead[way]},
         )
 
@@ -351,8 +362,8 @@
         return pltpu.make_async_remote_copy(
             src_ref=inn.at[slot],
             dst_ref=inn.at[slot],
-            send_sem=send.at[base + slot],
-            recv_sem=recv.at[base + slot],
+            send_sem=send.at[0],
+            recv_sem=recv.at[base + way * (outer - 1) + k],
             device_id={axis: block(0, 0, 0)},
         )
 
@@ -399,14 +410,17 @@
         def _(way=way):
             arrived(way, 0).wait_recv()
             acc[0] += inn[way * outer].astype(F32)
-    for j in range(1, inner):
-        across(j, 0, 0).wait_send()
-    for way, k in hops:
-        @pl.when(exists(way, k))
-        def _(way=way, k=k):
-            for j in range(1, inner):
-                across(j, way, k).wait_send()
-            along(way, k).wait_send()
+    drain(axis, block(0, 0, 0), near, (inner - 1) * outer + outer - 1, send, recv)
+
+
+def drain(axis, me, ref, count, send, recv):
+    pltpu.make_async_remote_copy(
+        src_ref=ref.at[pl.ds(0, count)],
+        dst_ref=ref.at[pl.ds(0, count)],
+        send_sem=send.at[0],
+        recv_sem=recv.at[0],
+        device_id={axis: me},
+    ).wait_send()
 
 
 def reduce_wide(axis, n, inner, place, acc, near, out, inn, send, recv):
@@ -419,8 +433,8 @@
         return pltpu.make_async_remote_copy(
             src_ref=place(block(way, k, j)) if first else out.at[slot],
             dst_ref=inn.at[slot - inner],
-            send_sem=send.at[base + slot],
-            recv_sem=recv.at[base + slot - inner],
+            send_sem=send.at[0],
+            recv_sem=recv.at[base + (way * (outer - 1) + k - 1) * inner + j],
             device_id={axis: ahead[way]},
         )
 
@@ -429,8 +443,8 @@
         return pltpu.make_async_remote_copy(
             src_ref=inn.at[slot],
             dst_ref=inn.at[slot],
-            send_sem=send.at[base + slot],
-            recv_sem=recv.at[base + slot],
+            send_sem=send.at[0],
+            recv_sem=recv.at[base + (way * (outer - 1) + k) * inner + j],
             device_id={axis: block(0, 0, 0)},
         )
 
@@ -438,7 +452,7 @@
         return pltpu.make_async_remote_copy(
             src_ref=out.at[j],
             dst_ref=near.at[j - 1],
-            send_sem=send.at[j - 1],
+            send_sem=send.at[0],
             recv_sem=recv.at[j - 1],
             device_id={axis: block(0, 0, j)},
         )
@@ -480,16 +494,7 @@
     for j in range(1, inner):
         across(j).wait_recv()
         acc[0] += near[j - 1].astype(F32)
-        across(j).wait_send()
-    for way, k in hops:
-        for first, test in ((True, starts), (False, fed)):
-            if k == outer - 1 and not first:
-                continue
-
-            @pl.when(jnp.logical_and(exists(way, k), test(way)))
-            def _(way=way, k=k, first=first):
-                for j in range(inner):
-                    along(way, k, j, first).wait_send()
+    drain(axis, block(0, 0, 0), inn, (outer - 1) * inner + inner - 1, send, recv)
 
 
 def reduce(route, *args):
@@ -498,16 +503,16 @@
 
 def reduce_scratch(n, inner, block, route=NEAR):
     outer = n // inner
-    near, slots, sums = (inner - 1) * 2 * outer, 2 * outer, 1
+    near, slots, sums, sems = (inner - 1) * 2 * outer, 2 * outer, 1, (inner - 1) * (2 * outer - 1) + 2 * (outer - 1)
     if route == WIDE:
-        near, slots, sums = inner - 1, 2 * outer * inner, inner
+        near, slots, sums, sems = inner - 1, 2 * outer * inner, inner, inner - 1 + 2 * (outer - 1) * inner
     return [
         pltpu.VMEM((sums,) + block, F32),
         pltpu.VMEM((near,) + block, BF16),
         pltpu.VMEM((slots,) + block, BF16),
         pltpu.VMEM((slots,) + block, BF16),
-        pltpu.SemaphoreType.DMA((near + slots,)),
-        pltpu.SemaphoreType.DMA((near + slots,)),
+        pltpu.SemaphoreType.DMA((1,)),
+        pltpu.SemaphoreType.DMA((sems,)),
     ]
 
 
@@ -544,8 +549,27 @@
     return sorted(pieces, key=lambda piece: -piece[2])
 
 
-def rows_of(ref, size, at, part):
-    return lambda block: ref.at[pl.ds(pl.multiple_of(block * size + at, math.gcd(size, at)), part), :]
+class rows_of:
+    def __init__(self, ref, size, at, part):
+        self.ref, self.size, self.at, self.part = ref, size, at, part
+
+    def __call__(self, block):
+        at = pl.multiple_of(block * self.size + self.at, math.gcd(self.size, self.at))
+        return self.ref.at[pl.ds(at, self.part), :]
+
+    def span(self, count):
+        return self.ref.at[pl.ds(0, count * self.part), :]
+
+
+class slots_of:
+    def __init__(self, ref):
+        self.ref = ref
+
+    def __call__(self, block):
+        return self.ref.at[block]
+
+    def span(self, count):
+        return self.ref.at[pl.ds(0, count)]
 
 
 def take(scratch, count):
@@ -567,12 +591,13 @@
     return ((0, 0, units, NEAR), (1, 0, units, NEAR), (2, 0, units // 2, WIDE), (2, units // 2, units // 2, NEAR))
 
 
-def forward_kernel(row, col, gate_ref, up_ref, down_ref, x_ref, src_out, dst_out, feats, down_all, hidden,
+def forward_kernel(row, col, units, in_ref, src_out, dst_out, feats, down_all, hidden,
                    gate_fac, up_fac, gate_all, up_all, branch, own_sem, *scratch):
     scratch = list(scratch)
-    units, size = gate_ref.shape[0], x_ref.shape[0]
+    size = in_ref.shape[0] - 3 * units
+    x_ref = in_ref.at[pl.ds(0, size), :]
     whole = (gate_all, up_all, down_all)
-    mine = (gate_ref, up_ref, down_ref)
+    mine = [in_ref.at[pl.ds(size + kind * units, units), :] for kind in range(3)]
     at_row, at_col = lax.axis_index("row"), lax.axis_index("col")
     local = [
         pltpu.make_async_copy(mine[kind], rows_of(whole[kind], units, 0, units)(at_col), own_sem.at[kind])
@@ -584,7 +609,7 @@
     greet((("row", row), ("col", col)))
     early, late = [], []
     for kind, at, part, route in unit_spans(units):
-        src = mine[kind].at[pl.ds(at, part), :]
+        src = in_ref.at[pl.ds(size + kind * units + at, part), :]
         steps = gather(route, "col", *col, src, rows_of(whole[kind], units, at, part), *take(scratch, 2))
         (late if kind == 2 else early).append(steps)
     early.append(gather(NEAR, "row", *row, x_ref, rows_of(feats, size, 0, size), *take(scratch, 2)))
@@ -637,13 +662,13 @@
     tot_row[at_row] = tot_ref[...]
 
     def totals(row_sems, col_sems):
-        yield from gather(NEAR, "row", *row, tot_row.at[at_row], lambda block: tot_row.at[block], *row_sems)
+        yield from gather(NEAR, "row", *row, tot_row.at[at_row], slots_of(tot_row), *row_sems)
         total = tot_row[0]
         for n in range(1, row[0]):
             total = total + tot_row[n]
         tot_col[at_col] = total
         yield
-        yield from gather(NEAR, "col", *col, tot_col.at[at_col], lambda block: tot_col.at[block], *col_sems)
+        yield from gather(NEAR, "col", *col, tot_col.at[at_col], slots_of(tot_col), *col_sems)
 
     def chain(at, part, route, col_refs, row_refs, row_sems):
         yield from together(
@@ -682,6 +707,18 @@
                 advance(running[-1:])
     loss_out[...] = jnp.broadcast_to(total[0:1, :] / (total[1:2, :] * BLOCK * BLOCK), loss_out.shape)
     finish(*running)
+
+
+def last_kernel(loss_ref, gate_ref, up_ref, down_ref, loss_out, gate_out, up_out, down_out, sems):
+    copies = [
+        pltpu.make_async_copy(src, dst, sems.at[n])
+        for n, (src, dst) in enumerate(((gate_ref, gate_out), (up_ref, up_out), (down_ref, down_out)))
+    ]
+    for copy in copies:
+        copy.start()
+    loss_out[0, 0] = jnp.max(loss_ref[...])
+    for copy in copies:
+        copy.wait()
 
 
 def per_device(row, col, node_feats, w_gate, w_up, w_down, tile_src, tile_dst, tile_mask, tile_count):
@@ -699,7 +736,7 @@
     for _, part, route in ahead(pieces):
         scratch += reduce_scratch(*row, (part, width)) + gather_sems(*col, route) + gather_sems(*row)
     src_rows, dst_rows, *saved = pl.pallas_call(
-        functools.partial(forward_kernel, row, col),
+        functools.partial(forward_kernel, row, col, units),
         out_shape=(
             shaped((col[0] * size, width), BF16),
             shaped((nodes, width), BF16),
@@ -709,12 +746,12 @@
             shaped((nodes, wide), F32),
             shaped((nodes, wide), F32),
         ),
-        in_specs=[hbm] * 4,
+        in_specs=[vmem],
         out_specs=(vmem,) * 7,
         scratch_shapes=scratch,
         compiler_params=pltpu.CompilerParams(collective_id=0, has_side_effects=True, vmem_limit_bytes=32 << 20),
         name="forward",
-    )(w_gate.T, w_up.T, w_down, node_feats)
+    )(jnp.concatenate((node_feats, w_gate.T, w_up.T, w_down)))
     src_part, dst_part, loss_part = tiles(src_rows, dst_rows, tile_src, tile_dst, tile_mask, tile_count)
     tots = loss_part.shape
     scratch = [pltpu.VMEM((nodes, width), BF16), pltpu.VMEM((nodes, wide), BF16), pltpu.VMEM((nodes, wide), BF16)]
@@ -735,6 +772,15 @@
         compiler_params=pltpu.CompilerParams(collective_id=1, has_side_effects=True, vmem_limit_bytes=44 << 20),
         name="backward",
     )(src_part, dst_part, loss_part, *saved)
+    loss, gate, up, down = pl.pallas_call(
+        last_kernel,
+        out_shape=(shaped((1, 1), F32),) + (shaped((units, width), F32),) * 3,
+        in_specs=[vmem] * 4,
+        out_specs=(pl.BlockSpec(memory_space=pltpu.SMEM), hbm, hbm, hbm),
+        scratch_shapes=[pltpu.SemaphoreType.DMA((3,))],
+        compiler_params=pltpu.CompilerParams(vmem_limit_bytes=2 << 20),
+        name="last",
+    )(loss, gate, up, down)
     return (loss[0, 0], gate.T, up.T, down)
 
 

time: 146 us -> 136 us (0.932)
  local copies, waits for them, and re-layouts: 7.24 us -> 0 us
  Pallas kernels: 137 us -> 133 us
  other arithmetic: 0 us -> 1.77 us
    unnamed x15 -> x0, local copies, waits for them, and re-layouts: 6.73 us -> none
    pallas_call x1, Pallas kernels: 55 us -> 52.6 us  [per_device(): pl.pallas_call(functools.partial(backward_kernel, row, col, 0.5 * width *...]
    pallas_call x1 -> x2, Pallas kernels: 55.1 us -> 54.5 us  [the longest x1 53.2 us: per_device(): pl.pallas_call(functools.partial(forward_kernel, row, col, units), out_sh...]
where the time goes in v2:
time: 136 us
  Pallas kernels  133 us (98%)
  other arithmetic  1.77 us (1%)
    pallas_call x1, Pallas kernels, per_device(): pl.pallas_call(functools.partial(forward_kernel, row, col, units), out_sh...  53.2 us
    pallas_call x1, Pallas kernels, per_device(): pl.pallas_call(functools.partial(backward_kernel, row, col, 0.5 * width *...  52.6 us
    pallas_call x1, Pallas kernels, tiles(): pl.pallas_call(functools.partial(tile_kernel, 0.5 * width ** (-0.5)), out...  26.1 us

profile of v2, /device:TPU:0, one launch (start us, length us, event | category | flops | bytes accessed | tf_op | source)
XLA Modules:
  0.0 136.2 jit_solution(8979986486885741379)
XLA Ops:
  1.3 0.7 pad_add_fusion.ids
  2.0 1.1 pad_maximum_fusion.in_ref
  3.1 53.2 %forward.1 = (bf16[2048,512]{1,0:T(8,128)(2,1)S(1)}, bf16[1024,512]{1,0:T(8,128)(2,1)S(1)}, bf16[1024,512]{1,0:T(8,128)(2,1)S(1)}, bf16[512,512]{1,0:T(8,128)(2,...) custom-call(bf16[448,512]{1,0:T(8,128)(2,1)S(1)} %pad_maximum_fusion.in_ref), custom_call_target="tpu_custom_call" | custom-call | tf_op jit(solution)/shard_map/forward/pallas_call | solution.py:738
  56.2 26.1 %tiles.1 = (bf16[2048,512]{1,0:T(8,128)(2,1)S(1)}, bf16[1024,512]{1,0:T(8,128)(2,1)S(1)}, f32[8,128]{1,0:T(8,128)S(1)}) custom-call(s32[1]{0:T(128)S(6)} %copy.12.count_ref, s32[2,16]{1,0:T(2,128)S(1)} %pad_add_fusion.ids, bf16[2048,512]{1,0:T(8,128)(2,1)S(1)} %get-tuple-element.22.src_ref, bf16[1024,512]{1,0:T(8,128)(2,1)S(1)} %get-tuple-element.23.dst_ref, ...), custom_call_target="tpu_custom_call" | custom-call | tf_op jit(solution)/shard_map/tiles/pallas_call | solution.py:81
  82.3 52.6 %backward.1 = (f32[8,128]{1,0:T(8,128)S(1)}, f32[64,512]{1,0:T(8,128)S(1)}, f32[64,512]{1,0:T(8,128)S(1)}, f32[64,512]{1,0:T(8,128)S(1)}) custom-call(bf16[2048,512]{1,0:T(8,128)(2,1)S(1)} %get-tuple-element.24.src_ref, bf16[1024,512]{1,0:T(8,128)(2,1)S(1)} %get-tuple-element.25.dst_ref, f32[8,128]{1,0:T(8,128)S(1)} %get-tuple-element.26.tot_ref, ...), custom_call_target="tpu_custom_call" | custom-call | tf_op jit(solution)/shard_map/backward/pallas_call | solution.py:766
  134.9 1.3 last.1
